TPU v7x, 256 devices: a whole 4x4x8 slice. The times are simulated.
256 devices in a mesh: row: 64 (over y, z, core), col: 4 (over x).
Axes of the slice: x: 4, y: 4, z: 8, core: 2. Of those that a mesh axis runs over, the one named last changes fastest.
Arguments:
- features: bfloat16 [65536, 256], P('row', 'col'), may hold values from -600 to 600
- tile_vals: bfloat16 [10240, 128, 128], P('row'), may hold values from -0.125 to 0.125
- tile_rows: int32 [64, 160], P('row'), may hold values from 0 to 7
- tile_srcs: int32 [64, 160], P('row'), may hold values from 0 to 135, as said below
- tile_count: int32 [64], P('row'), may hold values from 20 to 160, as said below
- needed: int32 [64, 64, 2], P('row'), may hold values from 0 to 7, as said below
- hop_noise: float32 [2, 65536, 256], P(None, 'row', 'col'), may hold values from -0.24 to 0.24
- enc_weight: bfloat16 [3, 256, 256], replicated, may hold values from -3.59375 to 3.59375
Outputs:
- encoded: bfloat16 [65536, 256], P('row', 'col')
Inputs may be any that keep to these rules, and one draw needn't show every extreme that they name: `tile_count`: some row index has exactly 160 live slots; slots at or beyond a row index's count are ignored. `tile_srcs`: A value s below 8 names the row index's own block s; otherwise s = 8 + o * 2 + c names entry c of needed for owner o, and o is never the row index itself. needed[d, o, :] are 2 distinct block indices among owner o's 8 blocks.
All inputs are finite; a program needn't handle non-finite values.
Results may differ from a plain program's by a relative error of at most 0.0053.
Values may be sent and summed in bfloat16 or wider, within the bound.
No kernel may reach another device: no remote copies, remote signals or barrier semaphores. Data moves between devices by JAX's collectives and lax.ppermute only.
A program may use at most 64 MiB of HBM per device.

v0:
```python
import jax
import jax.numpy as jnp
from jax import lax
from jax.sharding import PartitionSpec as P

BLK = 128
BPD = 8
TPD = 160
CAP = 2
HOPS = 2
epsilon = 1e-06


def shards(features, tile_vals, tile_rows, tile_srcs, tile_count, needed, hop_noise, enc_weight):
    row_count = lax.axis_size("row")
    row_index = lax.axis_index("row")
    col_index = lax.axis_index("col")
    local_rows, local_width = features.shape
    sources = tile_srcs[0]
    block_rows = tile_rows[0]
    live_count = tile_count[0]
    wanted = needed[0]
    tile_order = jnp.arange(TPD, dtype=jnp.int32)
    onehot = (
        (block_rows[:, None] == jnp.arange(BPD, dtype=jnp.int32)[None, :])
        & (tile_order < live_count)[:, None]
    ).astype(jnp.float32)

    def normalize(values):
        squares = lax.psum(jnp.sum(values * values, axis=1), "col")
        return (values / jnp.sqrt(squares + epsilon)[:, None]).astype(jnp.bfloat16)

    remote = jnp.maximum(sources - BPD, 0)
    slot_table = wanted.reshape(-1)
    looked_up = jnp.sum(
        jnp.where(
            remote[:, None] == jnp.arange(row_count * CAP, dtype=jnp.int32)[None, :],
            slot_table[None, :],
            0,
        ),
        axis=1,
    )
    global_block = jnp.where(
        sources < BPD, row_index * BPD + sources, remote // CAP * BPD + looked_up
    )
    current = normalize(features.astype(jnp.float32))
    layers = [current]
    for hop_index in range(HOPS):
        whole = lax.all_gather(current.reshape(BPD, BLK * local_width), "row", axis=0, tiled=True)
        products = jnp.einsum(
            "tij,tjf->tif",
            tile_vals,
            jnp.take(whole, global_block, axis=0).reshape(TPD, BLK, local_width),
            preferred_element_type=jnp.float32,
        )
        summed = jnp.einsum("tr,tif->rif", onehot, products, precision=lax.Precision.HIGHEST)
        current = normalize(summed.reshape(local_rows, local_width) + hop_noise[hop_index])
        layers.append(current)
    stacked = jnp.stack(layers)
    weight_slice = lax.dynamic_slice_in_dim(
        enc_weight, col_index * local_width, local_width, axis=1
    )
    terms = jnp.einsum("kri,kio->ro", stacked, weight_slice, preferred_element_type=jnp.float32)
    encoded = lax.psum_scatter(terms, "col", scatter_dimension=1, tiled=True)
    return encoded.astype(jnp.bfloat16)


def solution(mesh):
    in_specs = (
        P("row", "col"),
        P("row", None, None),
        P("row", None),
        P("row", None),
        P("row"),
        P("row", None, None),
        P(None, "row", "col"),
        P(),
    )
    out_specs = P("row", "col")
    return jax.shard_map(shards, mesh=mesh, in_specs=in_specs, out_specs=out_specs, check_vma=False)
```

profile of v0, /device:TPU:8, one launch (start us, length us, event | category | flops | bytes accessed | tf_op | source)
XLA Modules:
  0.0 299.7 jit_solution(14227140690207375910)
XLA Ops:
  6.5 1.0 fusion.9
  7.5 10.5 %psum.21 = f32[1024]{0:T(1024)S(1)} all-reduce(f32[1024]{0:T(1024)S(1)} %fusion.9), channel_id=1, replica_groups=mesh['row'=64,'col'=4] {'col'}, use_global_device_ids=true, to_apply=%region_1.2 | all-reduce | flops 1024 | bytes 8192 | tf_op jit(solution)/shard_map/psum | solution.py:30
  18.0 0.9 fusion.10
  19.2 0.9 reshape.66
  20.2 0.8 copy.14
  21.7 1.0 slice_bitcast_fusion.1
  22.7 0.8 copy.24
  23.5 0.5 iota_compare_fusion.2
  24.0 0.7 compare_reduce_fusion
  24.7 0.7 add_maximum_fusion
  25.6 77.1 %all-gather.3.cloned.1.call-done = bf16[512,8192]{1,0:T(8,128)(2,1)} async-done(((bf16[8,8192]{1,0:T(8,128)(2,1)}), bf16[512,8192]{1,0:T(8,128)(2,1)}) %all-gather.3.cloned.1.call-update) | async-done | bytes 8388624 | tf_op jit(solution)/shard_map/all_gather | solution.py:49
  102.7 9.0 %gather_fusion = bf16[160,8192]{1,0:T(8,128)(2,1)S(1)} fusion(bf16[512,8192]{1,0:T(8,128)(2,1)} %all-gather.3.cloned.1.call-done, s32[1024]{0:T(1024)S(1)} %pad_clamp_fusion), kind=kCustom, calls=%fused_computation.clone | custom fusion | bytes 5243520 | tf_op jit(solution)/shard_map/jit(_take)/gather | solution.py:53
  111.8 1.8 broadcast_select_fusion.1
  113.6 8.4 %reshape.67 = bf16[160,128,64]{2,1,0:T(8,128)(2,1)} reshape(bf16[160,8192]{1,0:T(8,128)(2,1)} %broadcast_select_fusion.1) | data formatting | bytes 5242880 | tf_op jit(solution)/shard_map/reshape | solution.py:53
  122.0 7.7 %convolution_bitcast_fusion.1 = f32[160,128,64]{1,2,0:T(8,128)S(1)} fusion(bf16[160,128,64]{2,1,0:T(8,128)(2,1)} %reshape.67, bf16[160,128,128]{2,1,0:T(8,128)(2,1)} %param.11), kind=kOutput, calls=%fused_computation.9 | convolution fusion | flops 335544320 | bytes 13107200 | tf_op jit(solution)/shard_map/tij,tjf->tif/dot_general | solution.py:50
  129.8 4.7 %fusion.14 = (f32[8,128]{1,0:T(8,128)S(1)}, f32[8,128,64]{1,0,2:T(8,128)S(1)}) fusion(f32[8,8,8,128]{3,2,1,0:T(8,128)S(1)} %copy-done.3, f32[160,128,64]{1,2,0:T(8,128)S(1)} %convolution_bitcast_fusion.1, s32[160]{0:T(256)S(1)} %bitcast.59, pred[160]{0:T(512)(128)(4,1)S(1)} %copy-done.8), kind=kOutput, calls=%fused_computation.25 | convolution fusion | flops 126027264 | bytes 5772064 | tf_op jit(solution)/shard_map/tr,tif->rif/dot_general | solution.py:56
  134.8 10.4 %psum.22 = f32[1024]{0:T(1024)S(1)} all-reduce(f32[1024]{0:T(1024)S(1)} %bitcast.55), channel_id=1, replica_groups=mesh['row'=64,'col'=4] {'col'}, use_global_device_ids=true, to_apply=%region_4.6 | all-reduce | flops 1024 | bytes 8192 | tf_op jit(solution)/shard_map/psum | solution.py:30
  145.2 0.7 divide_convert_fusion.2
  146.9 0.7 divide_convert_fusion.1
  147.6 0.3 reduce-scatter.2.cloned.1.call-start
  147.9 0.7 fusion.31
  148.6 0.8 copy.25
  149.4 76.1 %all-gather.5.cloned.1.call-done = bf16[512,8192]{1,0:T(8,128)(2,1)} async-done(((bf16[8,8192]{1,0:T(8,128)(2,1)}), bf16[512,8192]{1,0:T(8,128)(2,1)}) %all-gather.5.cloned.1.call-update) | async-done | bytes 8388624 | tf_op jit(solution)/shard_map/all_gather | solution.py:49
  225.4 9.0 %gather_fusion.1 = bf16[160,8192]{1,0:T(8,128)(2,1)S(1)} fusion(bf16[512,8192]{1,0:T(8,128)(2,1)} %all-gather.5.cloned.1.call-done, s32[1024]{0:T(1024)S(1)} %pad_clamp_fusion), kind=kCustom, calls=%fused_computation.1.clone | custom fusion | bytes 5243520 | tf_op jit(solution)/shard_map/jit(_take)/gather | solution.py:53
  234.5 1.8 broadcast_select_fusion
  236.3 8.4 %reshape.70 = bf16[160,128,64]{2,1,0:T(8,128)(2,1)} reshape(bf16[160,8192]{1,0:T(8,128)(2,1)} %broadcast_select_fusion) | data formatting | bytes 5242880 | tf_op jit(solution)/shard_map/reshape | solution.py:53
  244.7 7.7 %convolution_bitcast_fusion = f32[160,128,64]{1,2,0:T(8,128)S(1)} fusion(bf16[160,128,64]{2,1,0:T(8,128)(2,1)} %reshape.70, bf16[160,128,128]{2,1,0:T(8,128)(2,1)} %param.11), kind=kOutput, calls=%fused_computation.8 | convolution fusion | flops 335544320 | bytes 13107200 | tf_op jit(solution)/shard_map/tij,tjf->tif/dot_general | solution.py:50
  252.5 4.7 %fusion.12 = (f32[8,128]{1,0:T(8,128)S(1)}, f32[8,128,64]{1,0,2:T(8,128)S(1)}) fusion(f32[8,8,8,128]{3,2,1,0:T(8,128)S(1)} %copy-done.4, f32[160,128,64]{1,2,0:T(8,128)S(1)} %convolution_bitcast_fusion, s32[160]{0:T(256)S(1)} %bitcast.60, pred[160]{0:T(512)(128)(4,1)S(1)} %copy-done.9), kind=kOutput, calls=%fused_computation.22 | convolution fusion | flops 126027264 | bytes 5772064 | tf_op jit(solution)/shard_map/tr,tif->rif/dot_general | solution.py:56
  257.3 10.4 %psum.23 = f32[1024]{0:T(1024)S(1)} all-reduce(f32[1024]{0:T(1024)S(1)} %bitcast.56), channel_id=1, replica_groups=mesh['row'=64,'col'=4] {'col'}, use_global_device_ids=true, to_apply=%region_6.8 | all-reduce | flops 1024 | bytes 8192 | tf_op jit(solution)/shard_map/psum | solution.py:30
  267.8 1.3 convolution_bitcast_fusion.2
  269.1 22.4 %reduce-scatter.2.cloned.1.call-done = f32[1024,64]{0,1:T(8,128)} async-done(((f32[1024,256]{0,1:T(8,128)}), f32[1024,64]{0,1:T(8,128)}) %reduce-scatter.2.cloned.1.call-update) | async-done | bytes 262160 | tf_op jit(solution)/shard_map/reduce_scatter | solution.py:64
  291.5 1.6 convert_element_type.26
  (42 shorter events, 2.0 us)
Async XLA Ops:
  6.5 261.2 %copy-start = (bf16[3,256,256]{2,1,0:T(8,128)(2,1)S(1)}, bf16[3,256,256]{2,1,0:T(8,128)(2,1)}, u32[]{:S(2)}) copy-start(bf16[3,256,256]{2,1,0:T(8,128)(2,1)} %param.17) | copy-start | bytes 1179652
  6.5 96.2 %all-gather.3.cloned.1.call-start = ((), (), s32[]{:S(2)}) async-start(), calls=%async_computation.1 | async-start | bytes 8519680 | tf_op jit(solution)/shard_map/all_gather | solution.py:49
  20.1 205.3 %all-gather.5.cloned.1.call-start = ((), (), s32[]{:S(2)}) async-start(), calls=%async_computation.2 | async-start | bytes 8519680 | tf_op jit(solution)/shard_map/all_gather | solution.py:49
  122.0 7.7 %copy-start.3 = (f32[8,8,8,128]{3,2,1,0:T(8,128)S(1)}, f32[8,8,8,128]{3,2,1,0:T(8,128)}, u32[]{:S(2)}) copy-start(f32[8,8,8,128]{3,2,1,0:T(8,128)} %copy.24) | copy-start | bytes 786436
  122.0 7.7 %copy-start.7 = (s32[1,160]{1,0:T(1,128)S(1)}, s32[1,160]{1,0:T(1,128)}, u32[]{:S(2)}) copy-start(s32[1,160]{1,0:T(1,128)} %param.12) | copy-start | bytes 1924
  122.0 7.7 %copy-start.8 = (pred[160]{0:T(512)(128)(4,1)S(1)}, pred[160]{0:T(512)(128)(4,1)}, u32[]{:S(2)}) copy-start(pred[160]{0:T(512)(128)(4,1)} %iota_compare_fusion.2) | copy-start | bytes 484
  129.7 15.5 %copy-start.1 = (f32[2,1024,64]{1,2,0:T(8,128)S(1)}, f32[2,1024,64]{1,2,0:T(8,128)}, u32[]{:S(2)}) copy-start(f32[2,1024,64]{1,2,0:T(8,128)} %param.16) | copy-start | bytes 1572868
  129.8 18.2 %copy-start.2 = (bf16[1024,64]{0,1:T(8,128)(2,1)S(1)}, bf16[1024,64]{0,1:T(8,128)(2,1)}, u32[]{:S(2)}) copy-start(bf16[1024,64]{0,1:T(8,128)(2,1)} %param.10) | copy-start | bytes 393220
  147.6 143.9 %reduce-scatter.2.cloned.1.call-start = ((), (), s32[]{:S(2)}) async-start(), calls=%async_computation.3 | async-start | bytes 1310720 | tf_op jit(solution)/shard_map/reduce_scatter | solution.py:64
  244.7 7.7 %copy-start.4 = (f32[8,8,8,128]{3,2,1,0:T(8,128)S(1)}, f32[8,8,8,128]{3,2,1,0:T(8,128)}, u32[]{:S(2)}) copy-start(f32[8,8,8,128]{3,2,1,0:T(8,128)} %copy.25) | copy-start | bytes 786436
  244.7 7.7 %copy-start.9 = (pred[160]{0:T(512)(128)(4,1)S(1)}, pred[160]{0:T(512)(128)(4,1)}, u32[]{:S(2)}) copy-start(pred[160]{0:T(512)(128)(4,1)} %iota_compare_fusion.2) | copy-start | bytes 484
  252.4 15.3 %copy-start.5 = (bf16[1,1024,64]{1,2,0:T(8,128)(2,1)S(1)}, bf16[1,1024,64]{1,2,0:T(8,128)(2,1)}, u32[]{:S(2)}) copy-start(bf16[1,1024,64]{1,2,0:T(8,128)(2,1)} %fusion.31) | copy-start | bytes 393220
  252.4 15.3 %copy-start.6 = (bf16[1,1024,64]{1,2,0:T(8,128)(2,1)S(1)}, bf16[1,1024,64]{1,2,0:T(8,128)(2,1)}, u32[]{:S(2)}) copy-start(bf16[1,1024,64]{1,2,0:T(8,128)(2,1)} %get-tuple-element.8) | copy-start | bytes 393220
Sparse Core Ops, SparseCore 0:
  20.2 82.4 all-gather.2
  147.8 77.6 all-gather.4
  269.3 22.2 reduce-scatter.1
where the time goes:
time: 300 us
  waiting for transfers between devices  176 us (59%)
  local copies, waits for them, and re-layouts  40.7 us (14%)
  blocking collectives  31.4 us (10%)
  matrix products  26.2 us (9%)
  between operations  14 us (5%)
  other arithmetic  11.5 us (4%)
    all_gather x2, waiting for transfers between devices, shards(): lax.all_gather(current.reshape(BPD, BLK * local_width), 'row', axis=0, ti...  153 us
    psum x3, blocking collectives, normalize(): squares = lax.psum(jnp.sum(values * values, axis=1), 'col')  31.4 us
    reduce_scatter x1, waiting for transfers between devices, shards(): encoded = lax.psum_scatter(terms, 'col', scatter_dimension=1, tiled=True)  22.4 us
    gather x2, local copies, waits for them, and re-layouts, shards(): jnp.take(whole, global_block, axis=0).reshape(TPD, BLK, local_width)  18.1 us
    reshape x2, local copies, waits for them, and re-layouts, shards(): jnp.take(whole, global_block, axis=0).reshape(TPD, BLK, local_width)  16.8 us
    dot_general x2, matrix products, shards(): jnp.einsum('tij,tjf->tif', tile_vals, jnp.take(whole, global_block, axis=...  15.4 us
    dot_general x2, matrix products, shards(): jnp.einsum('tr,tif->rif', onehot, products, precision=lax.Precision.HIGHEST)  9.47 us
  transfers between devices with their start and end apart: 3, of which 3 were waited for; matrix products, arithmetic and copies ran while one was open for 2% of the time, Pallas kernels for 0%

commit v1 on v0

--- a/solution.py
+++ b/solution.py
@@ -27,7 +27,8 @@
     ).astype(jnp.float32)
 
     def normalize(values):
-        squares = lax.psum(jnp.sum(values * values, axis=1), "col")
+        x_part = jnp.sum(values * values, axis=1)
+        squares = lax.all_gather(x_part, "col").sum(axis=0)
         return (values / jnp.sqrt(squares + epsilon)[:, None]).astype(jnp.bfloat16)
 
     remote = jnp.maximum(sources - BPD, 0)

time: 300 us -> 311 us (1.037)
  blocking collectives: 31.4 us -> 37 us
  waiting for transfers between devices: 176 us -> 180 us
    all_gather x0 -> x3, blocking collectives: none -> 37 us  [normalize(): squares = lax.all_gather(x_part, 'col').sum(axis=0)]
    psum x3 -> x0, blocking collectives: 31.4 us -> none  [normalize(): squares = lax.psum(jnp.sum(values * values, axis=1), 'col')]
where the time goes in v1:
time: 311 us; the launch traced here: 310 us
  waiting for transfers between devices  180 us (58%)
  local copies, waits for them, and re-layouts  40.7 us (13%)
  blocking collectives  37 us (12%)
  matrix products  26.2 us (8%)
  between operations  14 us (5%)
  other arithmetic  11.5 us (4%)
    all_gather x2, waiting for transfers between devices, shards(): lax.all_gather(current.reshape(BPD, BLK * local_width), 'row', axis=0, ti...  156 us
    all_gather x3, blocking collectives, normalize(): squares = lax.all_gather(x_part, 'col').sum(axis=0)  37 us
    reduce_scatter x1, waiting for transfers between devices, shards(): encoded = lax.psum_scatter(terms, 'col', scatter_dimension=1, tiled=True)  23.9 us
    gather x2, local copies, waits for them, and re-layouts, shards(): jnp.take(whole, global_block, axis=0).reshape(TPD, BLK, local_width)  18.1 us
    reshape x2, local copies, waits for them, and re-layouts, shards(): jnp.take(whole, global_block, axis=0).reshape(TPD, BLK, local_width)  16.8 us
    dot_general x2, matrix products, shards(): jnp.einsum('tij,tjf->tif', tile_vals, jnp.take(whole, global_block, axis=...  15.4 us
    dot_general x2, matrix products, shards(): jnp.einsum('tr,tif->rif', onehot, products, precision=lax.Precision.HIGHEST)  9.47 us
  transfers between devices with their start and end apart: 3, of which 3 were waited for; matrix products, arithmetic and copies ran while one was open for 2% of the time, Pallas kernels for 0%

profile of v1, /device:TPU:8, one launch (start us, length us, event | category | flops | bytes accessed | tf_op | source)
XLA Modules:
  0.0 310.0 jit_solution(4673200169003570598)
XLA Ops:
  6.5 1.0 fusion.9
  7.5 12.4 %all-gather = f32[4096]{0:T(1024)S(1)} all-gather(f32[1024]{0:T(1024)S(1)} %fusion.9), channel_id=2, replica_groups=mesh['row'=64,'col'=4] {'col'}, dimensions={0}, use_global_device_ids=true | all-gather | bytes 20480 | tf_op jit(solution)/shard_map/all_gather | solution.py:31
  19.9 0.9 fusion.10
  21.1 0.9 reshape.86
  22.1 0.8 copy.22
  23.6 1.0 slice_bitcast_fusion.1
  24.6 0.8 copy.32
  25.4 0.5 iota_compare_fusion.2
  25.9 0.7 compare_reduce_fusion
  26.6 0.7 add_maximum_fusion
  27.5 78.7 %all-gather.6.cloned.1.call-done = bf16[512,8192]{1,0:T(8,128)(2,1)} async-done(((bf16[8,8192]{1,0:T(8,128)(2,1)}), bf16[512,8192]{1,0:T(8,128)(2,1)}) %all-gather.6.cloned.1.call-update) | async-done | bytes 8388624 | tf_op jit(solution)/shard_map/all_gather | solution.py:50
  106.2 9.0 %gather_fusion = bf16[160,8192]{1,0:T(8,128)(2,1)S(1)} fusion(bf16[512,8192]{1,0:T(8,128)(2,1)} %all-gather.6.cloned.1.call-done, s32[1024]{0:T(1024)S(1)} %pad_clamp_fusion), kind=kCustom, calls=%fused_computation.clone | custom fusion | bytes 5243520 | tf_op jit(solution)/shard_map/jit(_take)/gather | solution.py:54
  115.2 1.8 broadcast_select_fusion.1
  117.1 8.4 %reshape.87 = bf16[160,128,64]{2,1,0:T(8,128)(2,1)} reshape(bf16[160,8192]{1,0:T(8,128)(2,1)} %broadcast_select_fusion.1) | data formatting | bytes 5242880 | tf_op jit(solution)/shard_map/reshape | solution.py:54
  125.5 7.7 %convolution_bitcast_fusion.1 = f32[160,128,64]{1,2,0:T(8,128)S(1)} fusion(bf16[160,128,64]{2,1,0:T(8,128)(2,1)} %reshape.87, bf16[160,128,128]{2,1,0:T(8,128)(2,1)} %param.11), kind=kOutput, calls=%fused_computation.9 | convolution fusion | flops 335544320 | bytes 13107200 | tf_op jit(solution)/shard_map/tij,tjf->tif/dot_general | solution.py:51
  133.2 4.7 %fusion.14 = (f32[8,128]{1,0:T(8,128)S(1)}, f32[8,128,64]{1,0,2:T(8,128)S(1)}) fusion(f32[8,8,8,128]{3,2,1,0:T(8,128)S(1)} %copy-done.3, f32[160,128,64]{1,2,0:T(8,128)S(1)} %convolution_bitcast_fusion.1, s32[160]{0:T(256)S(1)} %bitcast.59, pred[160]{0:T(512)(128)(4,1)S(1)} %copy-done.8), kind=kOutput, calls=%fused_computation.25 | convolution fusion | flops 126027264 | bytes 5772064 | tf_op jit(solution)/shard_map/tr,tif->rif/dot_general | solution.py:57
  138.2 12.3 %all-gather.1 = f32[4,1,1024]{2,1,0:T(1,128)S(1)} all-gather(f32[1,1,1024]{2,1,0:T(1,128)S(1)} %bitcast.55), channel_id=1, replica_groups=mesh['row'=64,'col'=4] {'col'}, dimensions={0}, use_global_device_ids=true | all-gather | bytes 20480 | tf_op jit(solution)/shard_map/all_gather | solution.py:31
  150.6 0.7 divide_convert_fusion.2
  152.3 0.7 divide_convert_fusion.1
  153.0 0.3 reduce-scatter.2.cloned.1.call-start
  153.3 0.7 fusion.31
  154.0 0.8 copy.33
  154.7 77.6 %all-gather.8.cloned.1.call-done = bf16[512,8192]{1,0:T(8,128)(2,1)} async-done(((bf16[8,8192]{1,0:T(8,128)(2,1)}), bf16[512,8192]{1,0:T(8,128)(2,1)}) %all-gather.8.cloned.1.call-update) | async-done | bytes 8388624 | tf_op jit(solution)/shard_map/all_gather | solution.py:50
  232.4 9.0 %gather_fusion.1 = bf16[160,8192]{1,0:T(8,128)(2,1)S(1)} fusion(bf16[512,8192]{1,0:T(8,128)(2,1)} %all-gather.8.cloned.1.call-done, s32[1024]{0:T(1024)S(1)} %pad_clamp_fusion), kind=kCustom, calls=%fused_computation.1.clone | custom fusion | bytes 5243520 | tf_op jit(solution)/shard_map/jit(_take)/gather | solution.py:54
  241.4 1.8 broadcast_select_fusion
  243.2 8.4 %reshape.90 = bf16[160,128,64]{2,1,0:T(8,128)(2,1)} reshape(bf16[160,8192]{1,0:T(8,128)(2,1)} %broadcast_select_fusion) | data formatting | bytes 5242880 | tf_op jit(solution)/shard_map/reshape | solution.py:54
  251.6 7.7 %convolution_bitcast_fusion = f32[160,128,64]{1,2,0:T(8,128)S(1)} fusion(bf16[160,128,64]{2,1,0:T(8,128)(2,1)} %reshape.90, bf16[160,128,128]{2,1,0:T(8,128)(2,1)} %param.11), kind=kOutput, calls=%fused_computation.8 | convolution fusion | flops 335544320 | bytes 13107200 | tf_op jit(solution)/shard_map/tij,tjf->tif/dot_general | solution.py:51
  259.4 4.7 %fusion.12 = (f32[8,128]{1,0:T(8,128)S(1)}, f32[8,128,64]{1,0,2:T(8,128)S(1)}) fusion(f32[8,8,8,128]{3,2,1,0:T(8,128)S(1)} %copy-done.4, f32[160,128,64]{1,2,0:T(8,128)S(1)} %convolution_bitcast_fusion, s32[160]{0:T(256)S(1)} %bitcast.60, pred[160]{0:T(512)(128)(4,1)S(1)} %copy-done.9), kind=kOutput, calls=%fused_computation.22 | convolution fusion | flops 126027264 | bytes 5772064 | tf_op jit(solution)/shard_map/tr,tif->rif/dot_general | solution.py:57
  264.2 12.3 %all-gather.2 = f32[4,1,1024]{2,1,0:T(1,128)S(1)} all-gather(f32[1,1,1024]{2,1,0:T(1,128)S(1)} %bitcast.56), channel_id=1, replica_groups=mesh['row'=64,'col'=4] {'col'}, dimensions={0}, use_global_device_ids=true | all-gather | bytes 20480 | tf_op jit(solution)/shard_map/all_gather | solution.py:31
  276.6 1.3 convolution_bitcast_fusion.2
  278.0 23.9 %reduce-scatter.2.cloned.1.call-done = f32[1024,64]{0,1:T(8,128)} async-done(((f32[1024,256]{0,1:T(8,128)}), f32[1024,64]{0,1:T(8,128)}) %reduce-scatter.2.cloned.1.call-update) | async-done | bytes 262160 | tf_op jit(solution)/shard_map/reduce_scatter | solution.py:65
  301.8 1.6 convert_element_type.26
  (46 shorter events, 2.0 us)
Async XLA Ops:
  6.5 270.0 %copy-start = (bf16[3,256,256]{2,1,0:T(8,128)(2,1)S(1)}, bf16[3,256,256]{2,1,0:T(8,128)(2,1)}, u32[]{:S(2)}) copy-start(bf16[3,256,256]{2,1,0:T(8,128)(2,1)} %param.17) | copy-start | bytes 1179652
  6.5 99.7 %all-gather.6.cloned.1.call-start = ((), (), s32[]{:S(2)}) async-start(), calls=%async_computation.1 | async-start | bytes 8519680 | tf_op jit(solution)/shard_map/all_gather | solution.py:50
  22.0 210.3 %all-gather.8.cloned.1.call-start = ((), (), s32[]{:S(2)}) async-start(), calls=%async_computation.2 | async-start | bytes 8519680 | tf_op jit(solution)/shard_map/all_gather | solution.py:50
  125.5 7.7 %copy-start.3 = (f32[8,8,8,128]{3,2,1,0:T(8,128)S(1)}, f32[8,8,8,128]{3,2,1,0:T(8,128)}, u32[]{:S(2)}) copy-start(f32[8,8,8,128]{3,2,1,0:T(8,128)} %copy.32) | copy-start | bytes 786436
  125.5 7.7 %copy-start.7 = (s32[1,160]{1,0:T(1,128)S(1)}, s32[1,160]{1,0:T(1,128)}, u32[]{:S(2)}) copy-start(s32[1,160]{1,0:T(1,128)} %param.12) | copy-start | bytes 1924
  125.5 7.7 %copy-start.8 = (pred[160]{0:T(512)(128)(4,1)S(1)}, pred[160]{0:T(512)(128)(4,1)}, u32[]{:S(2)}) copy-start(pred[160]{0:T(512)(128)(4,1)} %iota_compare_fusion.2) | copy-start | bytes 484
  133.2 17.4 %copy-start.1 = (f32[2,1024,64]{1,2,0:T(8,128)S(1)}, f32[2,1024,64]{1,2,0:T(8,128)}, u32[]{:S(2)}) copy-start(f32[2,1024,64]{1,2,0:T(8,128)} %param.16) | copy-start | bytes 1572868
  133.2 20.1 %copy-start.2 = (bf16[1024,64]{0,1:T(8,128)(2,1)S(1)}, bf16[1024,64]{0,1:T(8,128)(2,1)}, u32[]{:S(2)}) copy-start(bf16[1024,64]{0,1:T(8,128)(2,1)} %param.10) | copy-start | bytes 393220
  153.0 148.8 %reduce-scatter.2.cloned.1.call-start = ((), (), s32[]{:S(2)}) async-start(), calls=%async_computation.3 | async-start | bytes 1310720 | tf_op jit(solution)/shard_map/reduce_scatter | solution.py:65
  251.6 7.7 %copy-start.4 = (f32[8,8,8,128]{3,2,1,0:T(8,128)S(1)}, f32[8,8,8,128]{3,2,1,0:T(8,128)}, u32[]{:S(2)}) copy-start(f32[8,8,8,128]{3,2,1,0:T(8,128)} %copy.33) | copy-start | bytes 786436
  251.6 7.7 %copy-start.9 = (pred[160]{0:T(512)(128)(4,1)S(1)}, pred[160]{0:T(512)(128)(4,1)}, u32[]{:S(2)}) copy-start(pred[160]{0:T(512)(128)(4,1)} %iota_compare_fusion.2) | copy-start | bytes 484
  259.3 17.2 %copy-start.5 = (bf16[1,1024,64]{1,2,0:T(8,128)(2,1)S(1)}, bf16[1,1024,64]{1,2,0:T(8,128)(2,1)}, u32[]{:S(2)}) copy-start(bf16[1,1024,64]{1,2,0:T(8,128)(2,1)} %fusion.31) | copy-start | bytes 393220
  259.4 17.2 %copy-start.6 = (bf16[1,1024,64]{1,2,0:T(8,128)(2,1)S(1)}, bf16[1,1024,64]{1,2,0:T(8,128)(2,1)}, u32[]{:S(2)}) copy-start(bf16[1,1024,64]{1,2,0:T(8,128)(2,1)} %get-tuple-element.8) | copy-start | bytes 393220
Sparse Core Ops, SparseCore 0:
  22.1 84.0 all-gather.5
  153.1 79.1 all-gather.7
  278.1 23.6 reduce-scatter.1
